TPU v7x, 256 devices: a whole 4x4x8 slice. The times are simulated.
256 devices in a mesh: expert: 32 (over z, y), etp: 8 (over x, core).
Axes of the slice: x: 4, y: 4, z: 8, core: 2. Of those that a mesh axis runs over, the one named last changes fastest.
Arguments:
- tokens: bfloat16 [32768, 2560], P(('expert', 'etp')), may hold values from -6 to 6
- grad_out: bfloat16 [32768, 2560], P(('expert', 'etp')), may hold values from -6 to 6
- router_weight: bfloat16 [2560, 32], replicated, may hold values from -0.125 to 0.125
- expert_choice: int32 [32768, 1], P(('expert', 'etp')), may hold values from 0 to 31; in each aligned block of 128 rows (0 to 127, 128 to 255, ...) at most 6 rows name the same one
- gate_pre: bfloat16 [32, 1536, 4096], P('expert', None, 'etp'), may hold values from -6 to 6
- up_pre: bfloat16 [32, 1536, 4096], P('expert', None, 'etp'), may hold values from -6 to 6
- w_gate: bfloat16 [32, 2560, 4096], P('expert', None, 'etp'), may hold values from -0.125 to 0.125
- w_up: bfloat16 [32, 2560, 4096], P('expert', None, 'etp'), may hold values from -0.125 to 0.125
- w_down: bfloat16 [32, 4096, 2560], P('expert', 'etp'), may hold values from -0.09375 to 0.09375
Outputs:
- token_grad: bfloat16 [32768, 2560], P(('expert', 'etp'))
- router_grad: float32 [2560, 32], replicated
Inputs may be any that keep to these rules, and one draw needn't show every extreme that they name: `expert_choice`: within the 128 tokens of one device no expert is chosen more than 6 times, and in every draw some expert is chosen exactly 6 times by the tokens of some device.
All inputs are finite; a program needn't handle non-finite values.
Results may differ from a plain program's by a relative error of at most 0.015.
Values may be sent and summed in bfloat16 or wider, within the bound.
No kernel may reach another device: no remote copies, remote signals or barrier semaphores. Data moves between devices by JAX's collectives and lax.ppermute only.
A program may use at most 128 MiB of HBM per device.

v0:
```python
import jax
import jax.numpy as jnp
from jax import lax
from jax.sharding import PartitionSpec as P


def local(tokens, grad_out, router_weight, expert_choice, gate_pre, up_pre, w_gate, w_up, w_down):
    width = tokens.shape[1]
    experts = router_weight.shape[1]
    n_expert = lax.axis_size("expert")
    n_etp = lax.axis_size("etp")
    capacity = gate_pre.shape[1] // (n_expert * n_etp)
    contract = (((1,), (1,)), ((), ()))
    chosen_ids = expert_choice[:, 0]
    picked = chosen_ids[:, None] == jnp.arange(experts, dtype=jnp.int32)[None, :]
    logits = jnp.dot(tokens, router_weight, preferred_element_type=jnp.float32)
    score = jax.nn.sigmoid(jnp.sum(jnp.where(picked, logits, 0.0), axis=1))
    counts = picked.astype(jnp.int32)
    earlier = jnp.cumsum(counts, axis=0) - counts
    position = jnp.sum(earlier * counts, axis=1)
    target = chosen_ids * capacity + position
    placed = jnp.arange(experts * capacity, dtype=jnp.int32)[:, None] == target[None, :]
    onehot = placed.astype(jnp.bfloat16)
    outgoing = jnp.dot(onehot, grad_out, preferred_element_type=jnp.float32).astype(jnp.bfloat16)
    own = lax.all_to_all(outgoing, "expert", split_axis=0, concat_axis=0, tiled=True)
    arrived = lax.all_gather(own, "etp", axis=0, tiled=True)
    d_hidden = lax.dot_general(arrived, w_down[0], contract, preferred_element_type=jnp.float32)
    gate_f = gate_pre[0].astype(jnp.float32)
    up_f = up_pre[0].astype(jnp.float32)
    sig = jax.nn.sigmoid(gate_f)
    d_gate = (d_hidden * up_f * sig * (1.0 + gate_f * (1.0 - sig))).astype(jnp.bfloat16)
    d_up = (d_hidden * gate_f * sig).astype(jnp.bfloat16)
    terms = (
        lax.dot_general(d_gate, w_gate[0], contract, preferred_element_type=jnp.float32)
        + lax.dot_general(d_up, w_up[0], contract, preferred_element_type=jnp.float32)
    ).astype(jnp.bfloat16)
    summed = lax.psum_scatter(terms, "etp", scatter_dimension=0, tiled=True)
    returned = lax.all_to_all(summed, "expert", split_axis=0, concat_axis=0, tiled=True)
    fetched = lax.dot_general(
        onehot, returned, (((0,), (0,)), ((), ())), preferred_element_type=jnp.float32
    )
    inputs = tokens.astype(jnp.float32)
    d_logit = jnp.sum(inputs * fetched, axis=1) * score * (1.0 - score)
    column = lax.dot_general(
        picked.astype(jnp.bfloat16), router_weight, contract, preferred_element_type=jnp.float32
    )
    token_grad = (score[:, None] * fetched + d_logit[:, None] * column).astype(jnp.bfloat16)
    weighted = jnp.where(picked, d_logit[:, None], 0.0)
    local_terms = lax.dot_general(
        weighted,
        inputs,
        (((0,), (0,)), ((), ())),
        precision=lax.Precision.HIGHEST,
        preferred_element_type=jnp.float32,
    )
    mine = lax.all_to_all(
        local_terms.reshape(n_etp, experts // n_etp, width),
        "etp",
        split_axis=0,
        concat_axis=0,
        tiled=True,
    )
    mine = jnp.sum(mine, axis=0)
    mine = lax.psum(mine, "expert")
    router_grad = lax.all_gather(mine, "etp", axis=0, tiled=True).T
    return (token_grad, router_grad)


def solution(mesh):
    placed = (
        P(("expert", "etp"), None),
        P(("expert", "etp"), None),
        P(),
        P(("expert", "etp"), None),
        P("expert", None, "etp"),
        P("expert", None, "etp"),
        P("expert", None, "etp"),
        P("expert", None, "etp"),
        P("expert", "etp", None),
    )
    return jax.shard_map(
        local,
        mesh=mesh,
        in_specs=placed,
        out_specs=(P(("expert", "etp"), None), P()),
        check_vma=False,
    )
```

profile of v0, /device:TPU:1, one launch (start us, length us, event | category | flops | bytes accessed | tf_op | source)
XLA Modules:
  0.0 423.1 jit_solution(13606596880845416231)
XLA Ops:
  7.2 0.0 copy-start
  7.2 0.0 all-gather.3.cloned.1.call-start
  7.2 0.8 fusion.29
  8.0 0.1 copy.15
  8.1 0.2 reduce_window_sum.11
  8.3 0.1 copy.16
  8.4 0.7 select_reduce_fusion
  9.1 0.7 multiply_add_fusion
  9.7 2.5 convolution_convert_fusion
  12.2 2.3 all_to_all.19
  14.4 46.0 %all_to_all.29 = bf16[32,6,2560]{2,1,0:T(8,128)(2,1)} all-to-all(bf16[32,6,2560]{2,1,0:T(8,128)(2,1)} %all_to_all.19), channel_id=1, replica_groups=mesh['expert'=32,'etp'=8] {'expert'}, dimensions={0} | all-to-all | bytes 1966080 | tf_op jit(solution)/shard_map/all_to_all | solution.py:25
  60.4 2.3 all_to_all.21
  62.7 0.0 all-gather.3.cloned.1.call-update
  62.7 0.0 reduce-scatter.2.cloned.1.call-start
  62.8 47.8 %all-gather.3.cloned.1.call-done = bf16[1536,2560]{1,0:T(8,128)(2,1)} async-done(((bf16[192,2560]{1,0:T(8,128)(2,1)}), bf16[1536,2560]{1,0:T(8,128)(2,1)}) %all-gather.3.cloned.1.call-update) | async-done | bytes 7864336 | tf_op jit(solution)/shard_map/all_gather | solution.py:26
  110.6 0.0 copy-start.4
  110.6 0.0 copy-start.5
  110.6 7.5 %fusion.14 = f32[1536,512]{1,0:T(8,128)S(1)} fusion(bf16[1536,2560]{1,0:T(8,128)(2,1)} %all-gather.3.cloned.1.call-done, bf16[1,512,2560]{2,1,0:T(8,128)(2,1)} %param.17), kind=kOutput, calls=%fused_computation.21 | convolution fusion | flops 4026531840 | bytes 13631488 | tf_op jit(solution)/shard_map/dot_general | solution.py:27
  118.1 0.0 copy-start.6
  118.1 1.7 copy-done.6
  119.8 0.0 copy-done
  119.8 0.0 copy-done.4
  119.8 0.0 copy-done.5
  119.8 9.8 %fusion.12 = f32[1536,2560]{1,0:T(8,128)} fusion(bf16[1,2560,512]{2,1,0:T(8,128)(2,1)S(1)} %copy-done, f32[1536,512]{1,0:T(8,128)S(1)} %fusion.14, bf16[1,1536,512]{2,1,0:T(8,128)(2,1)S(1)} %copy-done.4, bf16[1,1536,512]{2,1,0:T(8,128)(2,1)S(1)} %copy-done.5), kind=kOutput, calls=%fused_computation.19 | convolution fusion | flops 4035969024 | bytes 24641536 | tf_op jit(solution)/shard_map/dot_general | solution.py:34
  129.6 15.2 %add_convert_fusion = bf16[1536,2560]{1,0:T(8,128)(2,1)} fusion(f32[1536,2560]{1,0:T(8,128)} %fusion.12, bf16[1,2560,512]{2,1,0:T(8,128)(2,1)} %param.16, f32[1536,512]{1,0:T(8,128)} %copy-done.6, bf16[1,1536,512]{2,1,0:T(8,128)(2,1)} %param.13), kind=kOutput, calls=%fused_computation | convolution fusion | flops 4039901184 | bytes 30932992 | tf_op jit(solution)/shard_map/dot_general | solution.py:35
  144.9 0.0 reduce-scatter.2.cloned.1.call-update
  144.9 0.0 copy-start.1
  144.9 0.0 copy-start.2
  144.9 0.0 copy-start.3
  144.9 51.8 %reduce-scatter.2.cloned.1.call-done = bf16[192,2560]{1,0:T(8,128)(2,1)} async-done(((bf16[1536,2560]{1,0:T(8,128)(2,1)}), bf16[192,2560]{1,0:T(8,128)(2,1)}) %reduce-scatter.2.cloned.1.call-update) | async-done | bytes 983056 | tf_op jit(solution)/shard_map/reduce_scatter | solution.py:37
  196.8 2.3 all_to_all.22
  199.0 9.7 %all-to-all-start.1 = ((bf16[32,6,2560]{2,1,0:T(8,128)(2,1)}), bf16[32,6,2560]{2,1,0:T(8,128)(2,1)}, u32[]{:S(2)}, u32[]{:S(2)}) async-start(bf16[32,6,2560]{2,1,0:T(8,128)(2,1)} %all_to_all.22), calls=%async_computation.2 | async-start | bytes 2621440 | tf_op jit(solution)/shard_map/all_to_all | solution.py:38
  208.7 0.0 copy-done.1
  208.7 0.0 copy-done.2
  208.8 0.0 copy-done.3
  208.8 0.3 fusion.23
  209.1 30.4 %all-to-all-done.1 = bf16[32,6,2560]{2,1,0:T(8,128)(2,1)} async-done(((bf16[32,6,2560]{2,1,0:T(8,128)(2,1)}), bf16[32,6,2560]{2,1,0:T(8,128)(2,1)}, u32[]{:S(2)}, u32[]{:S(2)}) %all-to-all-start.1) | async-done | bytes 983072 | tf_op jit(solution)/shard_map/all_to_all | solution.py:38
  239.5 2.2 all_to_all.24
  241.7 2.7 multiply_reduce_fusion
  244.4 1.1 fusion.27
  245.5 1.8 reshape.36
  247.3 7.3 %all-to-all-start.2 = ((f32[8,4,2560]{2,1,0:T(4,128)}), f32[8,4,2560]{2,1,0:T(4,128)S(1)}, u32[]{:S(2)}, u32[]{:S(2)}) async-start(f32[8,4,2560]{2,1,0:T(4,128)} %reshape.36), calls=%async_computation.3 | async-start | bytes 655360 | tf_op jit(solution)/shard_map/all_to_all | solution.py:56
  254.6 2.5 fusion.1
  257.1 4.6 %all-to-all-done.2 = f32[8,4,2560]{2,1,0:T(4,128)S(1)} async-done(((f32[8,4,2560]{2,1,0:T(4,128)}), f32[8,4,2560]{2,1,0:T(4,128)S(1)}, u32[]{:S(2)}, u32[]{:S(2)}) %all-to-all-start.2) | async-done | bytes 327712 | tf_op jit(solution)/shard_map/all_to_all | solution.py:56
  261.7 0.1 reduce_sum.39
  261.8 112.4 %psum.7 = f32[4,2560]{1,0:T(4,128)S(1)} all-reduce(f32[4,2560]{1,0:T(4,128)S(1)} %reduce_sum.39), channel_id=1, replica_groups=mesh['expert'=32,'etp'=8] {'expert'}, use_global_device_ids=true, to_apply=%region_6.7 | all-reduce | flops 10240 | bytes 81920 | tf_op jit(solution)/shard_map/psum | solution.py:64
  374.2 41.3 %all-gather = f32[8,4,2560]{2,1,0:T(4,128)S(1)} all-gather(f32[1,4,2560]{2,1,0:T(4,128)S(1)} %bitcast.37), channel_id=1, replica_groups=mesh['expert'=32,'etp'=8] {'etp'}, dimensions={0}, use_global_device_ids=true | all-gather | bytes 368640 | tf_op jit(solution)/shard_map/all_gather | solution.py:65
  415.5 0.8 reshape.40
  (1 shorter events, 0.0 us)
Async XLA Ops:
  7.2 112.6 %copy-start = (bf16[1,2560,512]{2,1,0:T(8,128)(2,1)S(1)}, bf16[1,2560,512]{2,1,0:T(8,128)(2,1)}, u32[]{:S(2)}) copy-start(bf16[1,2560,512]{2,1,0:T(8,128)(2,1)} %param.15) | copy-start | bytes 7864324
  7.2 103.4 %all-gather.3.cloned.1.call-start = ((), (), s32[]{:S(2)}) async-start(), calls=%async_computation.4 | async-start | bytes 8847360 | tf_op jit(solution)/shard_map/all_gather | solution.py:26
  62.7 134.0 %reduce-scatter.2.cloned.1.call-start = ((), (), s32[]{:S(2)}) async-start(), calls=%async_computation.5 | async-start | bytes 8847360 | tf_op jit(solution)/shard_map/reduce_scatter | solution.py:37
  110.6 9.3 %copy-start.4 = (bf16[1,1536,512]{2,1,0:T(8,128)(2,1)S(1)}, bf16[1,1536,512]{2,1,0:T(8,128)(2,1)}, u32[]{:S(2)}) copy-start(bf16[1,1536,512]{2,1,0:T(8,128)(2,1)} %param.14) | copy-start | bytes 4718596
  110.6 9.3 %copy-start.5 = (bf16[1,1536,512]{2,1,0:T(8,128)(2,1)S(1)}, bf16[1,1536,512]{2,1,0:T(8,128)(2,1)}, u32[]{:S(2)}) copy-start(bf16[1,1536,512]{2,1,0:T(8,128)(2,1)} %param.13) | copy-start | bytes 4718596
  118.1 1.7 copy-start.6
  144.9 63.8 %copy-start.1 = (bf16[128,2560]{1,0:T(8,128)(2,1)S(1)}, bf16[128,2560]{1,0:T(8,128)(2,1)}, u32[]{:S(2)}) copy-start(bf16[128,2560]{1,0:T(8,128)(2,1)} %param.9) | copy-start | bytes 1966084
  144.9 63.8 %copy-start.2 = (bf16[2560,32]{0,1:T(8,128)(2,1)S(1)}, bf16[2560,32]{0,1:T(8,128)(2,1)}, u32[]{:S(2)}) copy-start(bf16[2560,32]{0,1:T(8,128)(2,1)} %param.11) | copy-start | bytes 491524
  144.9 63.8 %copy-start.3 = (s32[128,1]{0,1:T(1,128)S(1)}, s32[128,1]{0,1:T(1,128)}, u32[]{:S(2)}) copy-start(s32[128,1]{0,1:T(1,128)} %param.12) | copy-start | bytes 1540
  199.0 40.4 %all-to-all-start.1 = ((bf16[32,6,2560]{2,1,0:T(8,128)(2,1)}), bf16[32,6,2560]{2,1,0:T(8,128)(2,1)}, u32[]{:S(2)}, u32[]{:S(2)}) async-start(bf16[32,6,2560]{2,1,0:T(8,128)(2,1)} %all_to_all.22), calls=%async_computation.2 | async-start | bytes 2621440 | tf_op jit(solution)/shard_map/all_to_all | solution.py:38
  247.3 14.4 %all-to-all-start.2 = ((f32[8,4,2560]{2,1,0:T(4,128)}), f32[8,4,2560]{2,1,0:T(4,128)S(1)}, u32[]{:S(2)}, u32[]{:S(2)}) async-start(f32[8,4,2560]{2,1,0:T(4,128)} %reshape.36), calls=%async_computation.3 | async-start | bytes 655360 | tf_op jit(solution)/shard_map/all_to_all | solution.py:56
Sparse Core Ops, SparseCore 0:
  62.9 47.6 all-gather.2
  145.0 51.6 reduce-scatter.1
where the time goes:
time: 424 us; the launch traced here: 423 us
  blocking collectives  200 us (47%)
  waiting for transfers between devices  135 us (32%)
  matrix products  41.7 us (10%)
  starting transfers between devices  17.1 us (4%)
  between operations  14.1 us (3%)
  local copies, waits for them, and re-layouts  13.6 us (3%)
    psum x1, blocking collectives, local(): mine = lax.psum(mine, 'expert')  112 us
    reduce_scatter x1, waiting for transfers between devices, local(): summed = lax.psum_scatter(terms, 'etp', scatter_dimension=0, tiled=True)  51.8 us
    all_gather x1, waiting for transfers between devices, local(): arrived = lax.all_gather(own, 'etp', axis=0, tiled=True)  47.8 us
    all_to_all x1, blocking collectives, local(): lax.all_to_all(outgoing, 'expert', split_axis=0, concat_axis=0, tiled=True)  46 us
    all_gather x1, blocking collectives, local(): router_grad = lax.all_gather(mine, 'etp', axis=0, tiled=True).T  41.3 us
    all_to_all x1, waiting for transfers between devices, local(): lax.all_to_all(summed, 'expert', split_axis=0, concat_axis=0, tiled=True)  30.4 us
    dot_general x1, matrix products, local(): lax.dot_general(d_up, w_up[0], contract, preferred_element_type=jnp.float32)  15.2 us
    dot_general x1, matrix products, local(): lax.dot_general(d_gate, w_gate[0], contract, preferred_element_type=jnp.f...  9.81 us
  transfers between devices with their start and end apart: 4, of which 4 were waited for; matrix products, arithmetic and copies ran while one was open for 1% of the time, Pallas kernels for 0%

commit v1 on v0

--- a/solution.py
+++ b/solution.py
@@ -2,6 +2,28 @@
 import jax.numpy as jnp
 from jax import lax
 from jax.sharding import PartitionSpec as P
+from jax.lax import axis_index, axis_size, ppermute
+
+
+def _expand_files(row_axis, v0):
+    carry_in, view_out, g_now = (axis_size(row_axis), axis_index(row_axis), v0.shape[0])
+    chunks = tuple(((dev, (dev + 1) % carry_in) for dev in range(carry_in)))
+    grid = tuple(((dev, (dev - 1) % carry_in) for dev in range(carry_in)))
+    r1 = jnp.zeros((*v0.shape[:0], carry_in * g_now, *v0.shape[1:]), v0.dtype)
+    r1 = lax.dynamic_update_slice_in_dim(r1, v0, view_out * g_now, axis=0)
+    v_now = far_arr = v0
+    r_now = carry_in // 2
+    it = 1
+    while it < r_now + 1:
+        v_now = ppermute(v_now, axis_name=row_axis, perm=chunks)
+        r1 = lax.dynamic_update_slice_in_dim(r1, v_now, (view_out - it) % carry_in * g_now, axis=0)
+        if it < carry_in - r_now:
+            far_arr = ppermute(far_arr, row_axis, grid)
+            r1 = lax.dynamic_update_slice_in_dim(
+                r1, far_arr, (view_out + it) % carry_in * g_now, axis=0
+            )
+        it = it + 1
+    return r1
 
 
 def local(tokens, grad_out, router_weight, expert_choice, gate_pre, up_pre, w_gate, w_up, w_down):
@@ -62,7 +84,7 @@
     )
     mine = jnp.sum(mine, axis=0)
     mine = lax.psum(mine, "expert")
-    router_grad = lax.all_gather(mine, "etp", axis=0, tiled=True).T
+    router_grad = _expand_files("etp", mine).T
     return (token_grad, router_grad)
 
 

time: 424 us -> 426 us (level)
  blocking collectives: 200 us -> 158 us
  starting transfers between devices: 17.1 us -> 52.9 us
  waiting for transfers between devices: 135 us -> 142 us
    all_gather x1 -> x0, blocking collectives: 41.3 us -> none  [local(): router_grad = lax.all_gather(mine, 'etp', axis=0, tiled=True).T]
    ppermute x0 -> x7, starting transfers between devices: none -> 35.8 us  [the longest x4 33.1 us: _expand_files(): v_now = ppermute(v_now, axis_name=row_axis, perm=chunks)]
    ppermute x0 -> x7, waiting for transfers between devices: none -> 7.09 us  [the longest x4 6.23 us: _expand_files(): v_now = ppermute(v_now, axis_name=row_axis, perm=chunks)]
  transfers between devices with their start and end apart: 4 -> 11, of which waited for: 4 -> 11; matrix products, arithmetic and copies ran while one was open for 1% -> 1% of each run, Pallas kernels for 0% -> 0%
where the time goes in v1:
time: 426 us; the launch traced here: 424 us
  blocking collectives  158 us (37%)
  waiting for transfers between devices  142 us (33%)
  starting transfers between devices  52.9 us (12%)
  matrix products  41.5 us (10%)
  between operations  14.2 us (3%)
  local copies, waits for them, and re-layouts  13.7 us (3%)
    psum x1, blocking collectives, local(): mine = lax.psum(mine, 'expert')  112 us
    reduce_scatter x1, waiting for transfers between devices, local(): summed = lax.psum_scatter(terms, 'etp', scatter_dimension=0, tiled=True)  51.8 us
    all_gather x1, waiting for transfers between devices, local(): arrived = lax.all_gather(own, 'etp', axis=0, tiled=True)  47.8 us
    all_to_all x1, blocking collectives, local(): lax.all_to_all(outgoing, 'expert', split_axis=0, concat_axis=0, tiled=True)  46 us
    ppermute x4, starting transfers between devices, _expand_files(): v_now = ppermute(v_now, axis_name=row_axis, perm=chunks)  33.1 us
    all_to_all x1, waiting for transfers between devices, local(): lax.all_to_all(summed, 'expert', split_axis=0, concat_axis=0, tiled=True)  30.4 us
    dot_general x1, matrix products, local(): lax.dot_general(d_up, w_up[0], contract, preferred_element_type=jnp.float32)  15.2 us
    all_to_all x1, starting transfers between devices, local(): lax.all_to_all(summed, 'expert', split_axis=0, concat_axis=0, tiled=True)  9.68 us
  transfers between devices with their start and end apart: 11, of which 11 were waited for; matrix products, arithmetic and copies ran while one was open for 1% of the time, Pallas kernels for 0%

profile of v1, /device:TPU:1, one launch (start us, length us, event | category | flops | bytes accessed | tf_op | source)
XLA Modules:
  0.0 424.3 jit_solution(1007545511862666476)
XLA Ops:
  7.2 0.0 copy-start
  7.2 0.0 all-gather.2.cloned.1.call-start
  7.2 0.8 fusion.29
  8.0 0.1 copy.13
  8.1 0.2 reduce_window_sum.11
  8.3 0.1 copy.14
  8.4 0.7 select_reduce_fusion
  9.1 0.7 multiply_add_fusion
  9.7 2.4 convolution_convert_fusion
  12.2 2.3 all_to_all.19
  14.4 46.0 %all_to_all.29 = bf16[32,6,2560]{2,1,0:T(8,128)(2,1)} all-to-all(bf16[32,6,2560]{2,1,0:T(8,128)(2,1)} %all_to_all.19), channel_id=1, replica_groups=mesh['expert'=32,'etp'=8] {'expert'}, dimensions={0} | all-to-all | bytes 1966080 | tf_op jit(solution)/shard_map/all_to_all | solution.py:47
  60.4 2.3 all_to_all.21
  62.7 0.0 all-gather.2.cloned.1.call-update
  62.7 0.0 reduce-scatter.2.cloned.1.call-start
  62.8 47.8 %all-gather.2.cloned.1.call-done = bf16[1536,2560]{1,0:T(8,128)(2,1)} async-done(((bf16[192,2560]{1,0:T(8,128)(2,1)}), bf16[1536,2560]{1,0:T(8,128)(2,1)}) %all-gather.2.cloned.1.call-update) | async-done | bytes 7864336 | tf_op jit(solution)/shard_map/all_gather | solution.py:48
  110.5 0.0 copy-start.5
  110.5 0.0 copy-start.6
  110.6 7.5 %fusion.14 = f32[1536,512]{1,0:T(8,128)S(1)} fusion(bf16[1536,2560]{1,0:T(8,128)(2,1)} %all-gather.2.cloned.1.call-done, bf16[1,512,2560]{2,1,0:T(8,128)(2,1)} %param.17), kind=kOutput, calls=%fused_computation.21 | convolution fusion | flops 4026531840 | bytes 13631488 | tf_op jit(solution)/shard_map/dot_general | solution.py:49
  118.1 0.0 copy-start.7
  118.1 1.7 copy-done.7
  119.8 0.0 copy-done
  119.8 0.0 copy-done.5
  119.8 0.0 copy-done.6
  119.8 9.6 %fusion.12 = f32[1536,2560]{1,0:T(8,128)} fusion(bf16[1,2560,512]{2,1,0:T(8,128)(2,1)S(1)} %copy-done, f32[1536,512]{1,0:T(8,128)S(1)} %fusion.14, bf16[1,1536,512]{2,1,0:T(8,128)(2,1)S(1)} %copy-done.5, bf16[1,1536,512]{2,1,0:T(8,128)(2,1)S(1)} %copy-done.6), kind=kOutput, calls=%fused_computation.19 | convolution fusion | flops 4035969024 | bytes 24641536 | tf_op jit(solution)/shard_map/dot_general | solution.py:56
  129.4 15.2 %add_convert_fusion = bf16[1536,2560]{1,0:T(8,128)(2,1)} fusion(f32[1536,2560]{1,0:T(8,128)} %fusion.12, bf16[1,2560,512]{2,1,0:T(8,128)(2,1)} %param.16, f32[1536,512]{1,0:T(8,128)} %copy-done.7, bf16[1,1536,512]{2,1,0:T(8,128)(2,1)} %param.13), kind=kOutput, calls=%fused_computation | convolution fusion | flops 4039901184 | bytes 30932992 | tf_op jit(solution)/shard_map/dot_general | solution.py:57
  144.7 0.0 reduce-scatter.2.cloned.1.call-update
  144.7 0.0 copy-start.1
  144.7 0.0 copy-start.2
  144.7 0.0 copy-start.4
  144.7 51.8 %reduce-scatter.2.cloned.1.call-done = bf16[192,2560]{1,0:T(8,128)(2,1)} async-done(((bf16[1536,2560]{1,0:T(8,128)(2,1)}), bf16[192,2560]{1,0:T(8,128)(2,1)}) %reduce-scatter.2.cloned.1.call-update) | async-done | bytes 983056 | tf_op jit(solution)/shard_map/reduce_scatter | solution.py:59
  196.6 2.3 all_to_all.22
  198.8 9.7 %all-to-all-start.1 = ((bf16[32,6,2560]{2,1,0:T(8,128)(2,1)}), bf16[32,6,2560]{2,1,0:T(8,128)(2,1)}, u32[]{:S(2)}, u32[]{:S(2)}) async-start(bf16[32,6,2560]{2,1,0:T(8,128)(2,1)} %all_to_all.22), calls=%async_computation.2 | async-start | bytes 2621440 | tf_op jit(solution)/shard_map/all_to_all | solution.py:60
  208.5 0.0 copy-done.1
  208.5 0.0 copy-done.2
  208.5 0.0 copy-done.4
  208.5 0.3 fusion.23
  208.9 30.4 %all-to-all-done.1 = bf16[32,6,2560]{2,1,0:T(8,128)(2,1)} async-done(((bf16[32,6,2560]{2,1,0:T(8,128)(2,1)}), bf16[32,6,2560]{2,1,0:T(8,128)(2,1)}, u32[]{:S(2)}, u32[]{:S(2)}) %all-to-all-start.1) | async-done | bytes 983072 | tf_op jit(solution)/shard_map/all_to_all | solution.py:60
  239.2 2.3 all_to_all.24
  241.5 2.7 multiply_reduce_fusion
  244.2 1.1 fusion.27
  245.3 1.8 reshape.36
  247.1 7.3 %all-to-all-start.2 = ((f32[8,4,2560]{2,1,0:T(4,128)}), f32[8,4,2560]{2,1,0:T(4,128)S(1)}, u32[]{:S(2)}, u32[]{:S(2)}) async-start(f32[8,4,2560]{2,1,0:T(4,128)} %reshape.36), calls=%async_computation.3 | async-start | bytes 655360 | tf_op jit(solution)/shard_map/all_to_all | solution.py:78
  254.4 2.5 fusion.1
  256.9 4.6 %all-to-all-done.2 = f32[8,4,2560]{2,1,0:T(4,128)S(1)} async-done(((f32[8,4,2560]{2,1,0:T(4,128)}), f32[8,4,2560]{2,1,0:T(4,128)S(1)}, u32[]{:S(2)}, u32[]{:S(2)}) %all-to-all-start.2) | async-done | bytes 327712 | tf_op jit(solution)/shard_map/all_to_all | solution.py:78
  261.5 0.1 reduce_sum.39
  261.6 112.1 %psum.7 = f32[4,2560]{1,0:T(4,128)S(1)} all-reduce(f32[4,2560]{1,0:T(4,128)S(1)} %reduce_sum.39), channel_id=1, replica_groups=mesh['expert'=32,'etp'=8] {'expert'}, use_global_device_ids=true, to_apply=%region_6.7 | all-reduce | flops 10240 | bytes 81920 | tf_op jit(solution)/shard_map/psum | solution.py:86
  373.7 28.6 %collective-permute-start = (f32[4,2560]{1,0:T(4,128)S(1)}, f32[4,2560]{1,0:T(4,128)S(1)}, u32[]{:S(2)}, u32[]{:S(2)}) collective-permute-start(f32[4,2560]{1,0:T(4,128)S(1)} %psum.7), channel_id=1, source_target_pairs={{0,1},{1,2},{2,3},{3,4},{4,5},{5,6},{6,7},{7,0},{8,9},{9,10},{10,1... | collective-permute-start | bytes 122888 | tf_op jit(solution)/shard_map/ppermute | solution.py:18
  402.3 0.0 collective-permute-start.1
  402.3 1.0 collective-permute-done
  403.4 2.3 collective-permute-start.2
  405.7 0.3 collective-permute-done.1
  406.0 0.7 collective-permute-start.3
  406.8 0.7 collective-permute-done.2
  407.5 1.7 collective-permute-start.4
  409.1 0.3 collective-permute-done.3
  409.4 2.0 collective-permute-start.5
  411.4 0.7 collective-permute-done.4
  412.1 0.5 collective-permute-start.6
  412.6 0.3 collective-permute-done.5
  412.9 3.9 collective-permute-done.6
  416.7 0.0 copy-start.3
  416.8 0.7 copy-done.3
  (10 shorter events, 0.2 us)
Async XLA Ops:
  7.2 112.6 %copy-start = (bf16[1,2560,512]{2,1,0:T(8,128)(2,1)S(1)}, bf16[1,2560,512]{2,1,0:T(8,128)(2,1)}, u32[]{:S(2)}) copy-start(bf16[1,2560,512]{2,1,0:T(8,128)(2,1)} %param.15) | copy-start | bytes 7864324
  7.2 103.4 %all-gather.2.cloned.1.call-start = ((), (), s32[]{:S(2)}) async-start(), calls=%async_computation.4 | async-start | bytes 8847360 | tf_op jit(solution)/shard_map/all_gather | solution.py:48
  62.7 133.8 %reduce-scatter.2.cloned.1.call-start = ((), (), s32[]{:S(2)}) async-start(), calls=%async_computation.5 | async-start | bytes 8847360 | tf_op jit(solution)/shard_map/reduce_scatter | solution.py:59
  110.5 9.3 %copy-start.5 = (bf16[1,1536,512]{2,1,0:T(8,128)(2,1)S(1)}, bf16[1,1536,512]{2,1,0:T(8,128)(2,1)}, u32[]{:S(2)}) copy-start(bf16[1,1536,512]{2,1,0:T(8,128)(2,1)} %param.14) | copy-start | bytes 4718596
  110.5 9.3 %copy-start.6 = (bf16[1,1536,512]{2,1,0:T(8,128)(2,1)S(1)}, bf16[1,1536,512]{2,1,0:T(8,128)(2,1)}, u32[]{:S(2)}) copy-start(bf16[1,1536,512]{2,1,0:T(8,128)(2,1)} %param.13) | copy-start | bytes 4718596
  118.1 1.7 copy-start.7
  144.7 63.8 %copy-start.1 = (bf16[128,2560]{1,0:T(8,128)(2,1)S(1)}, bf16[128,2560]{1,0:T(8,128)(2,1)}, u32[]{:S(2)}) copy-start(bf16[128,2560]{1,0:T(8,128)(2,1)} %param.9) | copy-start | bytes 1966084
  144.7 63.8 %copy-start.2 = (bf16[2560,32]{0,1:T(8,128)(2,1)S(1)}, bf16[2560,32]{0,1:T(8,128)(2,1)}, u32[]{:S(2)}) copy-start(bf16[2560,32]{0,1:T(8,128)(2,1)} %param.11) | copy-start | bytes 491524
  144.7 63.8 %copy-start.4 = (s32[128,1]{0,1:T(1,128)S(1)}, s32[128,1]{0,1:T(1,128)}, u32[]{:S(2)}) copy-start(s32[128,1]{0,1:T(1,128)} %param.12) | copy-start | bytes 1540
  198.8 40.4 %all-to-all-start.1 = ((bf16[32,6,2560]{2,1,0:T(8,128)(2,1)}), bf16[32,6,2560]{2,1,0:T(8,128)(2,1)}, u32[]{:S(2)}, u32[]{:S(2)}) async-start(bf16[32,6,2560]{2,1,0:T(8,128)(2,1)} %all_to_all.22), calls=%async_computation.2 | async-start | bytes 2621440 | tf_op jit(solution)/shard_map/all_to_all | solution.py:60
  247.1 14.4 %all-to-all-start.2 = ((f32[8,4,2560]{2,1,0:T(4,128)}), f32[8,4,2560]{2,1,0:T(4,128)S(1)}, u32[]{:S(2)}, u32[]{:S(2)}) async-start(f32[8,4,2560]{2,1,0:T(4,128)} %reshape.36), calls=%async_computation.3 | async-start | bytes 655360 | tf_op jit(solution)/shard_map/all_to_all | solution.py:78
  373.7 29.7 %collective-permute-start = (f32[4,2560]{1,0:T(4,128)S(1)}, f32[4,2560]{1,0:T(4,128)S(1)}, u32[]{:S(2)}, u32[]{:S(2)}) collective-permute-start(f32[4,2560]{1,0:T(4,128)S(1)} %psum.7), channel_id=1, source_target_pairs={{0,1},{1,2},{2,3},{3,4},{4,5},{5,6},{6,7},{7,0},{8,9},{9,10},{10,1... | collective-permute-start | bytes 122888 | tf_op jit(solution)/shard_map/ppermute | solution.py:18
  402.3 3.7 collective-permute-start.1
  403.4 4.1 collective-permute-start.2
  406.0 3.4 collective-permute-start.3
  407.5 4.6 %collective-permute-start.4 = (f32[4,2560]{1,0:T(4,128)S(1)}, f32[4,2560]{1,0:T(4,128)S(1)}, u32[]{:S(2)}, u32[]{:S(2)}) collective-permute-start(f32[4,2560]{1,0:T(4,128)S(1)} %collective-permute-done.2), channel_id=1, source_target_pairs={{0,1},{1,2},{2,3},{3,4},{4,5},{5,6},{6,7},{7,0},{8,9},{9,10},{10,1... | collective-permute-start | bytes 122888 | tf_op jit(solution)/shard_map/ppermute | solution.py:18
  409.4 3.4 collective-permute-start.5
  412.1 4.6 %collective-permute-start.6 = (f32[4,2560]{1,0:T(4,128)S(1)}, f32[4,2560]{1,0:T(4,128)S(1)}, u32[]{:S(2)}, u32[]{:S(2)}) collective-permute-start(f32[4,2560]{1,0:T(4,128)S(1)} %collective-permute-done.4), channel_id=1, source_target_pairs={{0,1},{1,2},{2,3},{3,4},{4,5},{5,6},{6,7},{7,0},{8,9},{9,10},{10,1... | collective-permute-start | bytes 122888 | tf_op jit(solution)/shard_map/ppermute | solution.py:18
  416.7 0.7 copy-start.3
Sparse Core Ops, SparseCore 0:
  62.8 47.6 all-gather.1
  144.8 51.6 reduce-scatter.1
